TPU v7x, 32 devices: a whole 2x2x4 slice. The times are simulated.
32 devices in a mesh: energy: 16 (over z, y, x), space: 2 (over core).
Axes of the slice: x: 2, y: 2, z: 4, core: 2. Of those that a mesh axis runs over, the one named last changes fastest.
Arguments:
- lesser: bfloat16 [32, 2, 2, 256, 256], P('energy', 'space'), may hold values from -6 to 6
- greater: bfloat16 [32, 2, 2, 256, 256], P('energy', 'space'), may hold values from -6 to 6
- coulomb_diag: bfloat16 [2, 256, 256], P('space'), may hold values from -0.375 to 0.375
- coulomb_upper: bfloat16 [2, 256, 256], P('space'), may hold values from -0.375 to 0.375
Outputs:
- screened: bfloat16 [32, 2, 2, 256, 256], P('energy', 'space')
All inputs are finite; a program needn't handle non-finite values.
Results may differ from a plain program's by a relative error of at most 0.015.
Values may be sent and summed in bfloat16 or wider, within the bound.
A program may use at most 64 MiB of HBM per device.

v0:
```python
import math

import jax
import jax.numpy as jnp
from jax import lax
from jax.sharding import PartitionSpec as P


def from_behind(value, axis, steps):
    count = lax.axis_size(axis)
    leading, last = (max(0, -steps), min(count, count - steps))
    return lax.ppermute(value, axis, [(source, source + steps) for source in range(leading, last)])


def split_parts(values):
    high = values.astype(jnp.bfloat16)
    low = (values - high.astype(jnp.float32)).astype(jnp.bfloat16)
    return (high, low)


def product_two(table, data_bf):
    return jnp.dot(table[0], data_bf, preferred_element_type=jnp.float32) + jnp.dot(
        table[1], data_bf, preferred_element_type=jnp.float32
    )


def product_three(table, data_f32):
    data_high, data_low = split_parts(data_f32)
    total = jnp.dot(table[0], data_high, preferred_element_type=jnp.float32)
    total = total + jnp.dot(table[1], data_high, preferred_element_type=jnp.float32)
    return total + jnp.dot(table[0], data_low, preferred_element_type=jnp.float32)


def correlate(lesser_x, greater_x):
    energies = lesser_x.shape[0]
    length = 2 * energies
    tail_shape = lesser_x.shape[1:]

    def flatten(values, part):
        return values[:, :, part].reshape(energies, -1)

    lesser_re = flatten(lesser_x, 0)
    lesser_im = flatten(lesser_x, 1)
    greater_re = flatten(greater_x, 0)
    greater_im = flatten(greater_x, 1)
    freqs = lax.broadcasted_iota(jnp.int32, (length, energies), 0)
    places = lax.broadcasted_iota(jnp.int32, (length, energies), 1)
    angles = 2.0 * math.pi / length * jnp.mod(freqs * places, length).astype(jnp.float32)
    cosine = split_parts(jnp.cos(angles))
    sine = split_parts(jnp.sin(angles))
    cosine_t = split_parts(jnp.cos(angles).T)
    sine_t = split_parts(jnp.sin(angles).T)
    hat_lre = product_two(cosine, lesser_re) + product_two(sine, lesser_im)
    hat_lim = product_two(cosine, lesser_im) - product_two(sine, lesser_re)
    hat_gre = product_two(cosine, greater_re) - product_two(sine, greater_im)
    hat_gim = product_two(cosine, greater_im) + product_two(sine, greater_re)
    prod_re = hat_lre * hat_gre - hat_lim * hat_gim
    prod_im = hat_lre * hat_gim + hat_lim * hat_gre
    corr_re = (product_three(cosine_t, prod_re) - product_three(sine_t, prod_im)) / length
    corr_im = (product_three(cosine_t, prod_im) + product_three(sine_t, prod_re)) / length
    factor = jnp.float32(energies) ** (-0.5)
    shaped = (energies, tail_shape[0], tail_shape[2], tail_shape[3])
    real_part = (corr_im * factor).reshape(shaped)
    imag_part = (-corr_re * factor).reshape(shaped)
    return jnp.stack([real_part, imag_part], axis=2).astype(jnp.bfloat16)


def left_plain(coupler, blocks):
    return jnp.einsum("ab,ecbd->ecad", coupler, blocks, preferred_element_type=jnp.float32).astype(
        jnp.bfloat16
    )


def left_transposed(coupler, blocks):
    return jnp.einsum("ba,ecbd->ecad", coupler, blocks, preferred_element_type=jnp.float32).astype(
        jnp.bfloat16
    )


def right_transposed(left, coupler):
    return jnp.einsum("ecad,fd->ecaf", left, coupler, preferred_element_type=jnp.float32)


def right_plain(left, coupler):
    return jnp.einsum("ecad,df->ecaf", left, coupler, preferred_element_type=jnp.float32)


def per_device(lesser, greater, coulomb_diag, coulomb_upper):
    greater_t = jnp.swapaxes(greater, 3, 4)
    lesser_x, greater_x = (
        lax.all_to_all(lesser, "energy", split_axis=3, concat_axis=0, tiled=True),
        lax.all_to_all(greater_t, "energy", split_axis=3, concat_axis=0, tiled=True),
    )
    polar_x = correlate(lesser_x, greater_x)
    polar = lax.all_to_all(polar_x, "energy", split_axis=0, concat_axis=3, tiled=True)
    own = polar[:, 0]
    diag_block = coulomb_diag[0]
    upper_block = coulomb_upper[0]
    total = right_transposed(left_plain(diag_block, own), diag_block)
    polar_next = from_behind(polar, "space", -1)
    outgoing = right_plain(left_transposed(upper_block, own), upper_block)
    total = total + right_transposed(left_plain(upper_block, polar_next[:, 0]), upper_block)
    incoming = from_behind(outgoing.astype(jnp.bfloat16), "space", 1).astype(outgoing.dtype)
    total = total + incoming
    return total.astype(jnp.bfloat16)[:, None]


def solution(mesh):
    placed = (
        P("energy", "space", None, None, None),
        P("energy", "space", None, None, None),
        P("space", None, None),
        P("space", None, None),
    )
    return jax.shard_map(
        per_device,
        mesh=mesh,
        in_specs=placed,
        out_specs=P("energy", "space", None, None, None),
        check_vma=False,
    )
```

profile of v0, /device:TPU:1, one launch (start us, length us, event | category | flops | bytes accessed | tf_op | source)
XLA Modules:
  0.0 81.7 jit_solution(16510284216522427563)
XLA Ops:
  0.0 2.0 %copy.27 = bf16[2,1,2,256,256]{3,2,0,1,4:T(2,128)(2,1)} copy(bf16[2,1,2,256,256]{4,3,2,1,0:T(8,128)(2,1)} %param.5) | data formatting | bytes 1048576 | tf_op args[1]
  2.0 7.5 %all-to-all-start.1 = ((bf16[2,1,2,256,256]{4,2,0,1,3:T(2,128)(2,1)}), bf16[2,1,2,256,256]{4,2,0,1,3:T(2,128)(2,1)S(1)}, u32[]{:S(2)}, u32[]{:S(2)}) async-start(bf16[2,1,2,256,256]{4,2,0,1,3:T(2,128)(2,1)} %bitcast.3), calls=%async_computation.1 | async-start | bytes 1048576 | tf_op jit(solution)/shard_map/all_to_all | solution.py:92
  9.6 1.3 %copy.24 = bf16[2,1,2,256,256]{4,2,0,1,3:T(2,128)(2,1)} copy(bf16[2,1,2,256,256]{4,3,2,1,0:T(8,128)(2,1)S(1)} %copy-done.4) | data formatting | bytes 1048576 | tf_op args[0]
  10.9 11.0 %all-to-all-done.1 = bf16[2,1,2,256,256]{4,2,0,1,3:T(2,128)(2,1)S(1)} async-done(((bf16[2,1,2,256,256]{4,2,0,1,3:T(2,128)(2,1)}), bf16[2,1,2,256,256]{4,2,0,1,3:T(2,128)(2,1)S(1)}, u32[]{:S(2)}, u32[]{:S(2)}) %all-to-all-start.1) | async-done | bytes 524320 | tf_op jit(solution)/shard_map/all_to_all | solution.py:92
  21.9 6.0 %all-to-all-start = ((bf16[2,1,2,256,256]{4,2,0,1,3:T(2,128)(2,1)}), bf16[2,1,2,256,256]{4,2,0,1,3:T(2,128)(2,1)S(1)}, u32[]{:S(2)}, u32[]{:S(2)}) async-start(bf16[2,1,2,256,256]{4,2,0,1,3:T(2,128)(2,1)} %copy.24), calls=%async_computation | async-start | bytes 1048576 | tf_op jit(solution)/shard_map/all_to_all | solution.py:91
  28.1 0.1 copy.50
  28.2 0.1 copy.51
  28.3 0.4 fusion.44
  28.7 1.4 %fusion.48 = f32[64,4096]{1,0:T(8,128)} fusion(bf16[32,4096]{1,0:T(8,128)(2,1)S(1)} %bitcast.110), kind=kOutput, calls=%fused_computation.76 | convolution fusion | flops 16807936 | bytes 1310720 | tf_op jit(solution)/shard_map/dot_general | solution.py:22
  30.0 1.4 %fusion.52 = f32[64,4096]{1,0:T(8,128)} fusion(bf16[32,4096]{1,0:T(8,128)(2,1)S(1)} %bitcast.105), kind=kOutput, calls=%fused_computation.78 | convolution fusion | flops 16807936 | bytes 1310720 | tf_op jit(solution)/shard_map/dot_general | solution.py:22
  31.4 0.4 fusion.40
  31.8 8.0 %all-to-all-done = bf16[2,1,2,256,256]{4,2,0,1,3:T(2,128)(2,1)S(1)} async-done(((bf16[2,1,2,256,256]{4,2,0,1,3:T(2,128)(2,1)}), bf16[2,1,2,256,256]{4,2,0,1,3:T(2,128)(2,1)S(1)}, u32[]{:S(2)}, u32[]{:S(2)}) %all-to-all-start) | async-done | bytes 524320 | tf_op jit(solution)/shard_map/all_to_all | solution.py:91
  40.0 0.1 copy.49
  40.1 0.4 fusion.46
  40.5 0.4 fusion.50
  40.9 0.1 copy.48
  41.0 0.4 fusion.54
  41.4 0.4 fusion.42
  41.8 0.4 copy-done.2
  42.2 0.4 convolution_add_fusion.5
  42.6 0.4 convolution_add_fusion.7
  43.0 0.8 copy-done.1
  43.9 0.4 convolution_add_fusion.1
  44.3 0.4 convolution_add_fusion.3
  44.7 0.4 fusion.2
  45.1 0.4 fusion.3
  45.5 0.4 fusion
  45.9 0.6 multiply_add_fusion
  46.6 0.3 fusion.73
  46.8 0.3 fusion.64
  47.1 0.3 fusion.67
  47.4 0.3 fusion.70
  47.7 0.3 convolution_add_fusion.13
  48.0 0.3 convolution_add_fusion.15
  48.3 0.3 convolution_add_fusion.14
  48.6 0.3 fusion.11
  48.9 0.3 convolution_add_fusion.9
  49.2 0.3 convolution_add_fusion.11
  49.5 0.3 convolution_add_fusion.10
  49.8 0.3 fusion.10
  50.2 17.9 %all_to_all.54 = bf16[32,1,2,16,256]{4,3,2,1,0:T(8,128)(2,1)S(1)} all-to-all(bf16[32,1,2,16,256]{4,3,2,1,0:T(8,128)(2,1)S(1)} %pad_maximum_fusion), channel_id=1, replica_groups=mesh['energy'=16,'space'=2] {'energy'}, dimensions={0} | all-to-all | bytes 1048576 | tf_op jit(solution)/shard_map/all_to_all | solution.py:95
  68.1 0.2 copy.36
  68.3 6.3 %collective-permute-start = (bf16[2,1,2,256,256]{3,4,2,0,1:T(8,128)(2,1)S(1)}, bf16[2,1,2,256,256]{3,4,2,0,1:T(8,128)(2,1)S(1)}, u32[]{:S(2)}, u32[]{:S(2)}) collective-permute-start(bf16[2,1,2,256,256]{3,4,2,0,1:T(8,128)(2,1)S(1)} %copy.36), channel_id=1, source_target_pairs={{1,0},{3,2},{5,4},{7,6},{9,8},{11,10},{13,12},{15,14},{17,16},{19,... | collective-permute-start | bytes 1572872 | tf_op jit(solution)/shard_map/ppermute | solution.py:12
  74.7 1.6 %convolution_convert_fusion = bf16[2,2,256,256]{3,2,1,0:T(8,128)(2,1)} fusion(bf16[2,2,256,256]{3,2,1,0:T(8,128)(2,1)S(1)} %bitcast.122, bf16[1,256,256]{2,1,0:T(8,128)(2,1)S(1)} %copy-done), kind=kOutput, calls=%fused_computation.29 | convolution fusion | flops 268959744 | bytes 1179648 | tf_op jit(solution)/shard_map/ecad,df->ecaf/dot_general | solution.py:85
  76.3 1.3 %collective-permute-start.1 = (bf16[2,2,256,256]{3,2,1,0:T(8,128)(2,1)}, bf16[2,2,256,256]{3,2,1,0:T(8,128)(2,1)S(1)}, u32[]{:S(2)}, u32[]{:S(2)}) collective-permute-start(bf16[2,2,256,256]{3,2,1,0:T(8,128)(2,1)} %convolution_convert_fusion), channel_id=1, source_target_pairs={{0,1},{2,3},{4,5},{6,7},{8,9},{10,11},{12,13},{14,15},{16,17},{18,... | collective-permute-start | bytes 1572872 | tf_op jit(solution)/shard_map/ppermute | solution.py:12
  77.6 0.7 fusion.13
  78.3 2.0 %collective-permute-done.1 = bf16[2,2,256,256]{3,2,1,0:T(8,128)(2,1)S(1)} collective-permute-done((bf16[2,2,256,256]{3,2,1,0:T(8,128)(2,1)}, bf16[2,2,256,256]{3,2,1,0:T(8,128)(2,1)S(1)}, u32[]{:S(2)}, u32[]{:S(2)}) %collective-permute-start.1) | collective-permute-done | bytes 524320 | tf_op jit(solution)/shard_map/ppermute | solution.py:12
  80.3 1.5 %fusion.18 = bf16[2,1,2,256,256]{4,3,2,1,0:T(8,128)(2,1)} fusion(f32[2,2,256,256]{3,2,1,0:T(8,128)S(1)} %fusion.13, bf16[2,2,256,256]{3,2,1,0:T(8,128)(2,1)S(1)} %collective-permute-done.1, bf16[2,1,2,256,256]{3,4,2,0,1:T(8,128)(2,1)S(1)} %collective-permute-done, bf16[1,256,256]{2,1,0:T(8,128)(2,1)S(1)} %copy-done), kind=kOutput, calls=%fused_computation.39 | convolution fusion | flops 269746176 | bytes 2752512 | tf_op jit(solution)/shard_map/ecad,fd->ecaf/dot_general | solution.py:81
  (19 shorter events, 0.5 us)
Async XLA Ops:
  0.0 74.7 %copy-start = (bf16[1,256,256]{2,1,0:T(8,128)(2,1)S(1)}, bf16[1,256,256]{2,1,0:T(8,128)(2,1)}, u32[]{:S(2)}) copy-start(bf16[1,256,256]{2,1,0:T(8,128)(2,1)} %param.7) | copy-start | bytes 393220
  2.0 7.5 %copy-start.4 = (bf16[2,1,2,256,256]{4,3,2,1,0:T(8,128)(2,1)S(1)}, bf16[2,1,2,256,256]{4,3,2,1,0:T(8,128)(2,1)}, u32[]{:S(2)}) copy-start(bf16[2,1,2,256,256]{4,3,2,1,0:T(8,128)(2,1)} %param.4) | copy-start | bytes 1572868
  2.0 19.9 %all-to-all-start.1 = ((bf16[2,1,2,256,256]{4,2,0,1,3:T(2,128)(2,1)}), bf16[2,1,2,256,256]{4,2,0,1,3:T(2,128)(2,1)S(1)}, u32[]{:S(2)}, u32[]{:S(2)}) async-start(bf16[2,1,2,256,256]{4,2,0,1,3:T(2,128)(2,1)} %bitcast.3), calls=%async_computation.1 | async-start | bytes 1048576 | tf_op jit(solution)/shard_map/all_to_all | solution.py:92
  21.9 17.9 %all-to-all-start = ((bf16[2,1,2,256,256]{4,2,0,1,3:T(2,128)(2,1)}), bf16[2,1,2,256,256]{4,2,0,1,3:T(2,128)(2,1)S(1)}, u32[]{:S(2)}, u32[]{:S(2)}) async-start(bf16[2,1,2,256,256]{4,2,0,1,3:T(2,128)(2,1)} %copy.24), calls=%async_computation | async-start | bytes 1048576 | tf_op jit(solution)/shard_map/all_to_all | solution.py:91
  41.0 1.2 %copy-start.2 = (f32[64,4096]{1,0:T(8,128)S(1)}, f32[64,4096]{1,0:T(8,128)}, u32[]{:S(2)}) copy-start(f32[64,4096]{1,0:T(8,128)} %fusion.52) | copy-start | bytes 3145732
  42.6 1.2 %copy-start.1 = (f32[64,4096]{1,0:T(8,128)S(1)}, f32[64,4096]{1,0:T(8,128)}, u32[]{:S(2)}) copy-start(f32[64,4096]{1,0:T(8,128)} %fusion.48) | copy-start | bytes 3145732
  68.3 10.0 %collective-permute-start = (bf16[2,1,2,256,256]{3,4,2,0,1:T(8,128)(2,1)S(1)}, bf16[2,1,2,256,256]{3,4,2,0,1:T(8,128)(2,1)S(1)}, u32[]{:S(2)}, u32[]{:S(2)}) collective-permute-start(bf16[2,1,2,256,256]{3,4,2,0,1:T(8,128)(2,1)S(1)} %copy.36), channel_id=1, source_target_pairs={{1,0},{3,2},{5,4},{7,6},{9,8},{11,10},{13,12},{15,14},{17,16},{19,... | collective-permute-start | bytes 1572872 | tf_op jit(solution)/shard_map/ppermute | solution.py:12
  74.7 2.9 %copy-start.3 = (bf16[1,256,256]{2,1,0:T(8,128)(2,1)S(1)}, bf16[1,256,256]{2,1,0:T(8,128)(2,1)}, u32[]{:S(2)}) copy-start(bf16[1,256,256]{2,1,0:T(8,128)(2,1)} %param.6) | copy-start | bytes 393220
  76.3 4.0 %collective-permute-start.1 = (bf16[2,2,256,256]{3,2,1,0:T(8,128)(2,1)}, bf16[2,2,256,256]{3,2,1,0:T(8,128)(2,1)S(1)}, u32[]{:S(2)}, u32[]{:S(2)}) collective-permute-start(bf16[2,2,256,256]{3,2,1,0:T(8,128)(2,1)} %convolution_convert_fusion), channel_id=1, source_target_pairs={{0,1},{2,3},{4,5},{6,7},{8,9},{10,11},{12,13},{14,15},{16,17},{18,... | collective-permute-start | bytes 1572872 | tf_op jit(solution)/shard_map/ppermute | solution.py:12
where the time goes:
time: 82.4 us; the launch traced here: 81.7 us
  starting transfers between devices  21.1 us (26%)
  waiting for transfers between devices  21 us (25%)
  blocking collectives  17.9 us (22%)
  matrix products  15.8 us (19%)
  local copies, waits for them, and re-layouts  5.65 us (7%)
    all_to_all x1, blocking collectives, per_device(): lax.all_to_all(polar_x, 'energy', split_axis=0, concat_axis=3, tiled=True)  17.9 us
    all_to_all x1, waiting for transfers between devices, per_device(): lax.all_to_all(greater_t, 'energy', split_axis=3, concat_axis=0, tiled=True)  11 us
    all_to_all x1, waiting for transfers between devices, per_device(): lax.all_to_all(lesser, 'energy', split_axis=3, concat_axis=0, tiled=True)  8.03 us
    ppermute x2, starting transfers between devices, from_behind(): lax.ppermute(value, axis, [(source, source + steps) for source in range(l...  7.61 us
    all_to_all x1, starting transfers between devices, per_device(): lax.all_to_all(greater_t, 'energy', split_axis=3, concat_axis=0, tiled=True)  7.53 us
    all_to_all x1, starting transfers between devices, per_device(): lax.all_to_all(lesser, 'energy', split_axis=3, concat_axis=0, tiled=True)  5.98 us
    dot_general x8, matrix products, product_two(): jnp.dot(table[0], data_bf, preferred_element_type=jnp.float32)  5.1 us
    unnamed x18, local copies, waits for them, and re-layouts  5.07 us
  transfers between devices with their start and end apart: 4, of which 3 were waited for; matrix products, arithmetic and copies ran while one was open for 9% of the time, Pallas kernels for 0%

commit v1 on v0

--- a/solution.py
+++ b/solution.py
@@ -1,8 +1,11 @@
+import functools
 import math
 
 import jax
 import jax.numpy as jnp
 from jax import lax
+from jax.experimental import pallas as pl
+from jax.experimental.pallas import tpu as pltpu
 from jax.sharding import PartitionSpec as P
 
 
@@ -105,6 +108,270 @@
     return total.astype(jnp.bfloat16)[:, None]
 
 
+LAGS = 8
+STEPS = 4
+LANES = 128
+MESH = pl.DeviceIdType.MESH
+
+
+def to_energy(dest):
+    return {"energy": dest}
+
+
+def correlate_chunk(chunk, energies, lx, hx, lf, hf, cf, cx):
+    rows = lf.shape[2]
+    flat = (energies, rows, LANES)
+    for part_of, held in ((lx, lf), (hx, hf)):
+        re = part_of[chunk, :, :, 0].reshape(flat).astype(jnp.float32)
+        im = part_of[chunk, :, :, 1].reshape(flat).astype(jnp.float32)
+        held[0, pl.ds(0, energies)] = re
+        held[1, pl.ds(0, energies)] = im
+        held[2, pl.ds(0, energies)] = re + im
+    factor = float(energies) ** -0.5
+
+    def one_slab(slab, carry):
+        at = pl.ds(pl.multiple_of(slab * 8, 8), 8)
+        for first in range(0, energies, LAGS):
+            def step(turn, sums):
+                start = turn * STEPS
+                sums = list(sums)
+                for q in range(3):
+                    window = [lf[q, start + (first + t), at, :] for t in range(LAGS + STEPS - 1)]
+                    taps = [hf[q, start + u, at, :] for u in range(STEPS)]
+                    for u in range(STEPS):
+                        for j in range(LAGS):
+                            sums[q * LAGS + j] = sums[q * LAGS + j] + window[j + u] * taps[u]
+                return tuple(sums)
+
+            zero = jnp.zeros((8, LANES), jnp.float32)
+            sums = lax.fori_loop(0, (energies - first) // STEPS, step, (zero,) * (3 * LAGS))
+            for j in range(LAGS):
+                rr, ii, mixed = sums[j], sums[LAGS + j], sums[2 * LAGS + j]
+                cf[first + j, 0, at, :] = (mixed - rr - ii) * factor
+                cf[first + j, 1, at, :] = (ii - rr) * factor
+        return carry
+
+    lax.fori_loop(0, rows // 8, one_slab, 0)
+    cx[chunk] = cf[...].astype(jnp.bfloat16).reshape(cx.shape[1:])
+
+
+def kernel(
+    n, ns, lesser, greater, diag, upper, out,
+    gv, ht, lx, hx, lf, hf, cf, cx, polar, side, uprev, wside, total,
+    local_sem, send_sem, recv_l, recv_h, recv_p, side_send, side_recv, u_send, u_recv,
+):
+    me = lax.axis_index("energy")
+    row = lax.axis_index("space")
+    chunks, _, k, _, rows, _ = lx.shape
+    energies = n * k
+    has_next = row < ns - 1
+    has_prev = row > 0
+
+    barrier = pltpu.get_barrier_semaphore()
+
+    def greet(step, carry):
+        pl.semaphore_signal(
+            barrier, inc=1, device_id=to_energy(lax.rem(me + step, n)), device_id_type=MESH
+        )
+        return carry
+
+    lax.fori_loop(1, n, greet, 0)
+
+    @pl.when(has_next)
+    def _():
+        pl.semaphore_signal(barrier, inc=1, device_id={"space": row + 1}, device_id_type=MESH)
+
+    @pl.when(has_prev)
+    def _():
+        pl.semaphore_signal(barrier, inc=1, device_id={"space": row - 1}, device_id_type=MESH)
+
+    load = pltpu.make_async_copy(greater.at[:, 0], gv, local_sem.at[0])
+    load.start()
+
+    zeros = jnp.zeros((lf.shape[1] - energies,) + lf.shape[2:], jnp.float32)
+    for q in range(3):
+        lf[q, pl.ds(energies, lf.shape[1] - energies)] = zeros
+
+    pl.semaphore_wait(
+        barrier, n - 1 + has_next.astype(jnp.int32) + has_prev.astype(jnp.int32)
+    )
+
+    def scatter(source, held, c, kind, recv):
+        cols = pl.ds(c * LANES, LANES)
+
+        def part(dest):
+            return source.at[:, :, pl.ds(pl.multiple_of(dest * rows, rows), rows), cols]
+
+        def push(step, carry):
+            dest = lax.rem(me + step, n)
+            pltpu.make_async_remote_copy(
+                src_ref=part(dest), dst_ref=held.at[c, me], send_sem=send_sem.at[kind],
+                recv_sem=recv.at[c], device_id=to_energy(dest), device_id_type=MESH,
+            ).start()
+            return carry
+
+        lax.fori_loop(1, n, push, 0)
+        pltpu.make_async_copy(part(me), held.at[c, me], recv.at[c]).start()
+
+    u_copy = pltpu.make_async_remote_copy(
+        src_ref=upper.at[0], dst_ref=uprev, send_sem=u_send, recv_sem=u_recv,
+        device_id={"space": lax.rem(row + 1, ns)}, device_id_type=MESH,
+    )
+
+    @pl.when(has_next)
+    def _():
+        u_copy.start()
+
+    scatter(lesser.at[:, 0], lx, 0, 0, recv_l)
+    load.wait()
+    for e in range(k):
+        for part_at in range(2):
+            ht[e, part_at] = gv[e, part_at].T
+    scatter(ht, hx, 0, 1, recv_h)
+    for c in range(1, chunks):
+        scatter(lesser.at[:, 0], lx, c, 0, recv_l)
+        scatter(ht, hx, c, 1, recv_h)
+
+    wside[0] = upper[0]
+
+    @pl.when(has_prev)
+    def _():
+        u_copy.wait_recv()
+        wside[1] = uprev[...].T
+
+    def one_chunk(c, carry):
+        pltpu.make_async_copy(lx.at[c], lx.at[c], recv_l.at[c]).wait()
+        pltpu.make_async_copy(hx.at[c], hx.at[c], recv_h.at[c]).wait()
+        correlate_chunk(c, energies, lx, hx, lf, hf, cf, cx)
+        mine = pl.ds(pl.multiple_of(me * rows, rows), rows)
+
+        def push(step, carry_in):
+            dest = lax.rem(me + step, n)
+            pltpu.make_async_remote_copy(
+                src_ref=cx.at[c, dest], dst_ref=polar.at[c, :, :, mine, :],
+                send_sem=send_sem.at[2], recv_sem=recv_p.at[c],
+                device_id=to_energy(dest), device_id_type=MESH,
+            ).start()
+            return carry_in
+
+        lax.fori_loop(1, n, push, 0)
+        pltpu.make_async_copy(cx.at[c, me], polar.at[c, :, :, mine, :], recv_p.at[c]).start()
+        return carry
+
+    lax.fori_loop(0, chunks, one_chunk, 0)
+
+    def screen(block, coupler, slot, c, begin):
+        right = coupler[:, c * LANES:(c + 1) * LANES]
+        for e in range(k):
+            pair = jnp.concatenate([block[slot, e, 0], block[slot, e, 1]], axis=1)
+            left = jnp.dot(coupler, pair, preferred_element_type=jnp.float32).astype(jnp.bfloat16)
+            for part_at in range(2):
+                term = lax.dot_general(
+                    left[:, part_at * LANES:(part_at + 1) * LANES], right,
+                    (((1,), (1,)), ((), ())), preferred_element_type=jnp.float32,
+                )
+                if begin:
+                    total[e, part_at] = term
+                else:
+                    total[e, part_at] += term
+
+    def forward(c, slot, to):
+        return pltpu.make_async_remote_copy(
+            src_ref=polar.at[c], dst_ref=side.at[slot, c], send_sem=side_send.at[slot, c],
+            recv_sem=side_recv.at[slot, c], device_id={"space": to}, device_id_type=MESH,
+        )
+
+    up, down = lax.rem(row + 1, ns), lax.rem(row + ns - 1, ns)
+    for c in range(chunks):
+        pltpu.make_async_copy(polar.at[c], polar.at[c], recv_p.at[c]).wait()
+
+        @pl.when(has_prev)
+        def _():
+            forward(c, 0, down).start()
+
+        @pl.when(has_next)
+        def _():
+            forward(c, 1, up).start()
+
+        screen(polar, diag[0], c, c, c == 0)
+
+        @pl.when(has_next)
+        def _():
+            forward(c, 0, down).wait_recv()
+            screen(side.at[0], wside[0], c, c, False)
+
+        @pl.when(has_prev)
+        def _():
+            forward(c, 1, up).wait_recv()
+            screen(side.at[1], wside[1], c, c, False)
+
+    out[:, 0] = total[...].astype(jnp.bfloat16)
+
+    for c in range(chunks):
+        @pl.when(has_prev)
+        def _():
+            forward(c, 0, down).wait_send()
+
+        @pl.when(has_next)
+        def _():
+            forward(c, 1, up).wait_send()
+
+    @pl.when(has_next)
+    def _():
+        u_copy.wait_send()
+
+    for kind in range(3):
+        sent = lx.at[:, pl.ds(0, n - 1)]
+        pltpu.make_async_copy(sent, sent, send_sem.at[kind]).wait()
+
+
+def fused(n, ns, lesser, greater, diag, upper):
+    k, _, _, size, _ = lesser.shape
+    rows, chunks, energies = size // n, size // LANES, n * k
+    bf, f32 = jnp.bfloat16, jnp.float32
+    whole = (k, 2, size, size)
+    padded = energies + LAGS + STEPS
+    dma = pltpu.SemaphoreType.DMA
+    vmem = pl.BlockSpec(memory_space=pltpu.VMEM)
+    hbm = pl.BlockSpec(memory_space=pl.ANY)
+    return pl.pallas_call(
+        functools.partial(kernel, n, ns),
+        out_shape=jax.ShapeDtypeStruct(lesser.shape, bf),
+        in_specs=[hbm, hbm, vmem, vmem],
+        out_specs=vmem,
+        scratch_shapes=[
+            pltpu.VMEM(whole, bf),
+            pltpu.VMEM(whole, bf),
+            pltpu.VMEM((chunks, n, k, 2, rows, LANES), bf),
+            pltpu.VMEM((chunks, n, k, 2, rows, LANES), bf),
+            pltpu.VMEM((3, padded, rows, LANES), f32),
+            pltpu.VMEM((3, energies, rows, LANES), f32),
+            pltpu.VMEM((energies, 2, rows, LANES), f32),
+            pltpu.VMEM((chunks, n, k, 2, rows, LANES), bf),
+            pltpu.VMEM((chunks, k, 2, size, LANES), bf),
+            pltpu.VMEM((2, chunks, k, 2, size, LANES), bf),
+            pltpu.VMEM((size, size), bf),
+            pltpu.VMEM((2, size, size), bf),
+            pltpu.VMEM(whole, f32),
+            dma((1,)), dma((3,)), dma((chunks,)), dma((chunks,)), dma((chunks,)),
+            dma((2, chunks)), dma((2, chunks)), dma, dma,
+        ],
+        compiler_params=pltpu.CompilerParams(
+            collective_id=0, has_side_effects=True, vmem_limit_bytes=40 << 20
+        ),
+    )(lesser, greater, diag, upper)
+
+
+def fits(n, ns, size, energies):
+    return size % n == 0 and (size // n) % 16 == 0 and size % LANES == 0 and energies % LAGS == 0 and ns > 1
+
+
+def either(n, ns, lesser, greater, diag, upper):
+    if fits(n, ns, lesser.shape[3], n * lesser.shape[0]):
+        return fused(n, ns, lesser, greater, diag, upper)
+    return per_device(lesser, greater, diag, upper)
+
+
 def solution(mesh):
     placed = (
         P("energy", "space", None, None, None),
@@ -113,7 +380,7 @@
         P("space", None, None),
     )
     return jax.shard_map(
-        per_device,
+        functools.partial(either, mesh.shape["energy"], mesh.shape["space"]),
         mesh=mesh,
         in_specs=placed,
         out_specs=P("energy", "space", None, None, None),

time: 82.4 us -> 48.7 us (0.59)
  Pallas kernels: 0 us -> 43.8 us
  starting transfers between devices: 21.1 us -> 0 us
  waiting for transfers between devices: 21 us -> 0 us
  blocking collectives: 17.9 us -> 0 us
  matrix products: 15.8 us -> 0 us
  local copies, waits for them, and re-layouts: 5.65 us -> 4.69 us
    pallas_call x0 -> x1, Pallas kernels: none -> 43.8 us  [fused(): pl.pallas_call(functools.partial(kernel, n, ns), out_shape=jax.ShapeDtype...]
    all_to_all x2 -> x0, waiting for transfers between devices: 19 us -> none  [the longest x1 11 us: per_device(): lax.all_to_all(greater_t, 'energy', split_axis=3, concat_axis=0, tiled=True)]
    all_to_all x1 -> x0, blocking collectives: 17.9 us -> none  [per_device(): lax.all_to_all(polar_x, 'energy', split_axis=0, concat_axis=3, tiled=True)]
    dot_general x31 -> x0, matrix products: 15.8 us -> none  [the longest x8 5.1 us: product_two(): jnp.dot(table[0], data_bf, preferred_element_type=jnp.float32)]
    all_to_all x2 -> x0, starting transfers between devices: 13.5 us -> none  [the longest x1 7.53 us: per_device(): lax.all_to_all(greater_t, 'energy', split_axis=3, concat_axis=0, tiled=True)]
    ppermute x2 -> x0, starting transfers between devices: 7.61 us -> none  [from_behind(): lax.ppermute(value, axis, [(source, source + steps) for source in range(l...]
    ppermute x2 -> x0, waiting for transfers between devices: 1.97 us -> none  [from_behind(): lax.ppermute(value, axis, [(source, source + steps) for source in range(l...]
    unnamed x18 -> x9, local copies, waits for them, and re-layouts: 5.07 us -> 4.69 us
  transfers between devices with their start and end apart: 4 -> 0, of which waited for: 3 -> 0; matrix products, arithmetic and copies ran while one was open for 9% -> 0% of each run, Pallas kernels for 0% -> 0%
where the time goes in v1:
time: 48.7 us; the launch traced here: 48.5 us
  Pallas kernels  43.8 us (90%)
  local copies, waits for them, and re-layouts  4.69 us (10%)
    pallas_call x1, Pallas kernels, fused(): pl.pallas_call(functools.partial(kernel, n, ns), out_shape=jax.ShapeDtype...  43.8 us
    unnamed x9, local copies, waits for them, and re-layouts  4.69 us

profile of v1, /device:TPU:1, one launch (start us, length us, event | category | flops | bytes accessed | tf_op | source)
XLA Modules:
  0.0 48.5 jit_solution(3684577014685782641)
XLA Ops:
  0.0 0.0 copy-start
  0.0 1.0 %copy-done = bf16[2,1,2,256,256]{4,3,2,1,0:T(8,128)(2,1)S(1)} copy-done((bf16[2,1,2,256,256]{4,3,2,1,0:T(8,128)(2,1)S(1)}, bf16[2,1,2,256,256]{4,3,2,1,0:T(8,128)(2,1)}, u32[]{:S(2)}) %copy-start) | copy-done | bytes 524312
  1.0 0.0 copy-start.1
  1.0 1.0 %copy-done.1 = bf16[2,1,2,256,256]{4,3,2,1,0:T(8,128)(2,1)S(1)} copy-done((bf16[2,1,2,256,256]{4,3,2,1,0:T(8,128)(2,1)S(1)}, bf16[2,1,2,256,256]{4,3,2,1,0:T(8,128)(2,1)}, u32[]{:S(2)}) %copy-start.1) | copy-done | bytes 524312
  2.1 0.0 copy-start.2
  2.1 0.9 %copy-done.2 = bf16[1,256,256]{2,1,0:T(8,128)(2,1)S(1)} copy-done((bf16[1,256,256]{2,1,0:T(8,128)(2,1)S(1)}, bf16[1,256,256]{2,1,0:T(8,128)(2,1)}, u32[]{:S(2)}) %copy-start.2) | copy-done | bytes 131096
  3.0 0.0 copy-start.3
  3.0 0.9 %copy-done.3 = bf16[1,256,256]{2,1,0:T(8,128)(2,1)S(1)} copy-done((bf16[1,256,256]{2,1,0:T(8,128)(2,1)S(1)}, bf16[1,256,256]{2,1,0:T(8,128)(2,1)}, u32[]{:S(2)}) %copy-start.3) | copy-done | bytes 131096
  3.9 43.8 %shard_map.46 = bf16[2,1,2,256,256]{4,3,2,1,0:T(8,128)(2,1)S(1)} custom-call(bf16[2,1,2,256,256]{4,3,2,1,0:T(8,128)(2,1)S(1)} %copy-done, bf16[2,1,2,256,256]{4,3,2,1,0:T(8,128)(2,1)S(1)} %copy-done.1, bf16[1,256,256]{2,1,0:T(8,128)(2,1)S(1)} %copy-done.2, bf16[1,256,256]{2,1,0:T(8,128)(2,1)S(1)} %copy-done.3), custom_call_target="tpu_custom_call" | custom-call | tf_op jit(solution)/shard_map/pallas_call | solution.py:337
  47.7 0.8 %copy.6 = bf16[2,1,2,256,256]{4,3,2,1,0:T(8,128)(2,1)} copy(bf16[2,1,2,256,256]{4,3,2,1,0:T(8,128)(2,1)S(1)} %shard_map.46) | data formatting | bytes 1048576
Async XLA Ops:
  0.0 1.0 %copy-start = (bf16[2,1,2,256,256]{4,3,2,1,0:T(8,128)(2,1)S(1)}, bf16[2,1,2,256,256]{4,3,2,1,0:T(8,128)(2,1)}, u32[]{:S(2)}) copy-start(bf16[2,1,2,256,256]{4,3,2,1,0:T(8,128)(2,1)} %lesser.1) | copy-start | bytes 1572868
  1.0 1.0 %copy-start.1 = (bf16[2,1,2,256,256]{4,3,2,1,0:T(8,128)(2,1)S(1)}, bf16[2,1,2,256,256]{4,3,2,1,0:T(8,128)(2,1)}, u32[]{:S(2)}) copy-start(bf16[2,1,2,256,256]{4,3,2,1,0:T(8,128)(2,1)} %greater.1) | copy-start | bytes 1572868
  2.1 0.9 %copy-start.2 = (bf16[1,256,256]{2,1,0:T(8,128)(2,1)S(1)}, bf16[1,256,256]{2,1,0:T(8,128)(2,1)}, u32[]{:S(2)}) copy-start(bf16[1,256,256]{2,1,0:T(8,128)(2,1)} %diag.1) | copy-start | bytes 393220
  3.0 0.9 %copy-start.3 = (bf16[1,256,256]{2,1,0:T(8,128)(2,1)S(1)}, bf16[1,256,256]{2,1,0:T(8,128)(2,1)}, u32[]{:S(2)}) copy-start(bf16[1,256,256]{2,1,0:T(8,128)(2,1)} %upper.1) | copy-start | bytes 393220

commit v2 on v1

--- a/solution.py
+++ b/solution.py
@@ -156,8 +156,8 @@
 
 
 def kernel(
-    n, ns, lesser, greater, diag, upper, out,
-    gv, ht, lx, hx, lf, hf, cf, cx, polar, side, uprev, wside, total,
+    n, ns, lesser, greater, diag_hbm, upper_hbm, out,
+    diag, upper, gv, ht, lx, hx, lf, hf, cf, cx, polar, side, uprev, wside, total,
     local_sem, send_sem, recv_l, recv_h, recv_p, side_send, side_recv, u_send, u_recv,
 ):
     me = lax.axis_index("energy")
@@ -187,6 +187,14 @@
 
     load = pltpu.make_async_copy(greater.at[:, 0], gv, local_sem.at[0])
     load.start()
+    load_upper = pltpu.make_async_copy(upper_hbm, upper, local_sem.at[1])
+    load_upper.start()
+    load_diag = pltpu.make_async_copy(diag_hbm, diag, local_sem.at[2])
+    load_diag.start()
+    load.wait()
+    for e in range(k):
+        for part_at in range(2):
+            ht[e, part_at] = gv[e, part_at].T
 
     zeros = jnp.zeros((lf.shape[1] - energies,) + lf.shape[2:], jnp.float32)
     for q in range(3):
@@ -214,7 +222,7 @@
         pltpu.make_async_copy(part(me), held.at[c, me], recv.at[c]).start()
 
     u_copy = pltpu.make_async_remote_copy(
-        src_ref=upper.at[0], dst_ref=uprev, send_sem=u_send, recv_sem=u_recv,
+        src_ref=upper_hbm.at[0], dst_ref=uprev, send_sem=u_send, recv_sem=u_recv,
         device_id={"space": lax.rem(row + 1, ns)}, device_id_type=MESH,
     )
 
@@ -223,15 +231,13 @@
         u_copy.start()
 
     scatter(lesser.at[:, 0], lx, 0, 0, recv_l)
-    load.wait()
-    for e in range(k):
-        for part_at in range(2):
-            ht[e, part_at] = gv[e, part_at].T
     scatter(ht, hx, 0, 1, recv_h)
     for c in range(1, chunks):
         scatter(lesser.at[:, 0], lx, c, 0, recv_l)
         scatter(ht, hx, c, 1, recv_h)
 
+    load_upper.wait()
+    load_diag.wait()
     wside[0] = upper[0]
 
     @pl.when(has_prev)
@@ -333,13 +339,15 @@
     padded = energies + LAGS + STEPS
     dma = pltpu.SemaphoreType.DMA
     vmem = pl.BlockSpec(memory_space=pltpu.VMEM)
-    hbm = pl.BlockSpec(memory_space=pl.ANY)
+    hbm = pl.BlockSpec(memory_space=pltpu.HBM)
     return pl.pallas_call(
         functools.partial(kernel, n, ns),
         out_shape=jax.ShapeDtypeStruct(lesser.shape, bf),
-        in_specs=[hbm, hbm, vmem, vmem],
+        in_specs=[hbm] * 4,
         out_specs=vmem,
         scratch_shapes=[
+            pltpu.VMEM(diag.shape, bf),
+            pltpu.VMEM(upper.shape, bf),
             pltpu.VMEM(whole, bf),
             pltpu.VMEM(whole, bf),
             pltpu.VMEM((chunks, n, k, 2, rows, LANES), bf),
@@ -353,13 +361,13 @@
             pltpu.VMEM((size, size), bf),
             pltpu.VMEM((2, size, size), bf),
             pltpu.VMEM(whole, f32),
-            dma((1,)), dma((3,)), dma((chunks,)), dma((chunks,)), dma((chunks,)),
+            dma((3,)), dma((3,)), dma((chunks,)), dma((chunks,)), dma((chunks,)),
             dma((2, chunks)), dma((2, chunks)), dma, dma,
         ],
         compiler_params=pltpu.CompilerParams(
             collective_id=0, has_side_effects=True, vmem_limit_bytes=40 << 20
         ),
-    )(lesser, greater, diag, upper)
+    )(*(pltpu.with_memory_space_constraint(x, pltpu.HBM) for x in (lesser, greater, diag, upper)))
 
 
 def fits(n, ns, size, energies):

time: 48.7 us -> 44.9 us (0.922)
  local copies, waits for them, and re-layouts: 4.69 us -> 0.8 us
    unnamed x9 -> x1, local copies, waits for them, and re-layouts: 4.69 us -> 0.8 us
where the time goes in v2:
time: 44.9 us; the launch traced here: 44.8 us
  Pallas kernels  44 us (98%)
  local copies, waits for them, and re-layouts  0.8 us (2%)
    pallas_call x1, Pallas kernels, fused(): pl.pallas_call(functools.partial(kernel, n, ns), out_shape=jax.ShapeDtype...  44 us

profile of v2, /device:TPU:1, one launch (start us, length us, event | category | flops | bytes accessed | tf_op | source)
XLA Modules:
  0.0 44.8 jit_solution(16859329784258115424)
XLA Ops:
  0.0 44.0 %shard_map.46 = bf16[2,1,2,256,256]{4,3,2,1,0:T(8,128)(2,1)S(1)} custom-call(bf16[2,1,2,256,256]{4,3,2,1,0:T(8,128)(2,1)} %lesser.1, bf16[2,1,2,256,256]{4,3,2,1,0:T(8,128)(2,1)} %greater.1, bf16[1,256,256]{2,1,0:T(8,128)(2,1)} %diag_hbm.1, bf16[1,256,256]{2,1,0:T(8,128)(2,1)} %upper_hbm.1), custom_call_target="tpu_custom_call" | custom-call | tf_op jit(solution)/shard_map/pallas_call | solution.py:343
  44.0 0.8 %copy.6 = bf16[2,1,2,256,256]{4,3,2,1,0:T(8,128)(2,1)} copy(bf16[2,1,2,256,256]{4,3,2,1,0:T(8,128)(2,1)S(1)} %shard_map.46) | data formatting | bytes 1048576

commit v3 on v2

--- a/solution.py
+++ b/solution.py
@@ -118,15 +118,15 @@
     return {"energy": dest}
 
 
-def correlate_chunk(chunk, energies, lx, hx, lf, hf, cf, cx):
-    rows = lf.shape[2]
-    flat = (energies, rows, LANES)
-    for part_of, held in ((lx, lf), (hx, hf)):
-        re = part_of[chunk, :, :, 0].reshape(flat).astype(jnp.float32)
-        im = part_of[chunk, :, :, 1].reshape(flat).astype(jnp.float32)
-        held[0, pl.ds(0, energies)] = re
-        held[1, pl.ds(0, energies)] = im
-        held[2, pl.ds(0, energies)] = re + im
+def widen_into(held, at, re, im):
+    re, im = re.astype(jnp.float32), im.astype(jnp.float32)
+    held[0, at] = re
+    held[1, at] = im
+    held[2, at] = re + im
+
+
+def correlate_into(cf, lf, hf, bounds):
+    energies, _, rows, _ = cf.shape
     factor = float(energies) ** -0.5
 
     def one_slab(slab, carry):
@@ -144,7 +144,8 @@
                 return tuple(sums)
 
             zero = jnp.zeros((8, LANES), jnp.float32)
-            sums = lax.fori_loop(0, (energies - first) // STEPS, step, (zero,) * (3 * LAGS))
+            low, high = bounds(first)
+            sums = lax.fori_loop(low, high, step, (zero,) * (3 * LAGS))
             for j in range(LAGS):
                 rr, ii, mixed = sums[j], sums[LAGS + j], sums[2 * LAGS + j]
                 cf[first + j, 0, at, :] = (mixed - rr - ii) * factor
@@ -152,13 +153,13 @@
         return carry
 
     lax.fori_loop(0, rows // 8, one_slab, 0)
-    cx[chunk] = cf[...].astype(jnp.bfloat16).reshape(cx.shape[1:])
 
 
 def kernel(
     n, ns, lesser, greater, diag_hbm, upper_hbm, out,
     diag, upper, gv, ht, lx, hx, lf, hf, cf, cx, polar, side, uprev, wside, total,
-    local_sem, send_sem, recv_l, recv_h, recv_p, side_send, side_recv, u_send, u_recv,
+    lxb, hxb, lfb, hfb, cfb, cxb, partial,
+    local_sem, send_sem, recv_l, recv_h, recv_p, side_send, side_recv, u_send, u_recv, half_send, half_recv,
 ):
     me = lax.axis_index("energy")
     row = lax.axis_index("space")
@@ -166,6 +167,11 @@
     energies = n * k
     has_next = row < ns - 1
     has_prev = row > 0
+    peers = n // 2
+    half, member = me // peers, lax.rem(me, peers)
+    own_energies = peers * k
+    brows = lxb.shape[3]
+    upper_half, lower_half = half == 1, half == 0
 
     barrier = pltpu.get_barrier_semaphore()
 
@@ -199,6 +205,7 @@
     zeros = jnp.zeros((lf.shape[1] - energies,) + lf.shape[2:], jnp.float32)
     for q in range(3):
         lf[q, pl.ds(energies, lf.shape[1] - energies)] = zeros
+    lfb[...] = jnp.zeros(lfb.shape, jnp.float32)
 
     pl.semaphore_wait(
         barrier, n - 1 + has_next.astype(jnp.int32) + has_prev.astype(jnp.int32)
@@ -230,8 +237,31 @@
     def _():
         u_copy.start()
 
-    scatter(lesser.at[:, 0], lx, 0, 0, recv_l)
-    scatter(ht, hx, 0, 1, recv_h)
+    def spread(pick, land, at_half, begin, kind):
+        def push(step, carry):
+            peer = lax.rem(member + step, peers)
+            dest = at_half * peers + peer
+            pltpu.make_async_remote_copy(
+                src_ref=pick(dest, peer), dst_ref=land(me, member), send_sem=half_send.at[kind],
+                recv_sem=half_recv.at[kind], device_id=to_energy(dest), device_id_type=MESH,
+            ).start()
+            return carry
+
+        lax.fori_loop(begin, peers, push, 0)
+        if begin:
+            pltpu.make_async_copy(pick(me, member), land(me, member), half_recv.at[kind]).start()
+
+    def band(source):
+        return lambda dest, peer: source.at[
+            :, :, pl.ds(pl.multiple_of(peer * brows, brows), brows), pl.ds(0, LANES)
+        ]
+
+    @pl.when(lower_half)
+    def _():
+        spread(band(ht), lambda at, peer: hxb.at[at], 1, 0, 2)
+
+    spread(band(lesser.at[:, 0]), lambda at, peer: lxb.at[at], half, 1, 0)
+    spread(band(ht), lambda at, peer: hxb.at[at], half, 1, 1)
     for c in range(1, chunks):
         scatter(lesser.at[:, 0], lx, c, 0, recv_l)
         scatter(ht, hx, c, 1, recv_h)
@@ -245,10 +275,50 @@
         u_copy.wait_recv()
         wside[1] = uprev[...].T
 
+    def arrived(buffer, kind):
+        pltpu.make_async_copy(buffer, buffer, half_recv.at[kind]).wait()
+
+    some = pl.ds(0, peers)
+    own = pl.ds(half * peers, peers)
+    own_at = pl.ds(half * own_energies, own_energies)
+    short = (own_energies, brows, LANES)
+    arrived(lxb.at[some], 0)
+    widen_into(lfb, own_at, lxb[own, :, 0].reshape(short), lxb[own, :, 1].reshape(short))
+    arrived(hxb.at[some], 1)
+    widen_into(hfb, own_at, hxb[own, :, 0].reshape(short), hxb[own, :, 1].reshape(short))
+
+    @pl.when(upper_half)
+    def _():
+        arrived(hxb.at[some], 2)
+        widen_into(
+            hfb, pl.ds(0, own_energies), hxb[some, :, 0].reshape(short), hxb[some, :, 1].reshape(short)
+        )
+
+    def half_bounds(first):
+        begin = max(0, (own_energies - first - (LAGS + STEPS - 2)) // STEPS)
+        low_end, high_end = max(0, own_energies - first) // STEPS, (energies - first) // STEPS
+        return half * begin, low_end + half * (high_end - low_end)
+
+    correlate_into(cfb, lfb, hfb, half_bounds)
+    cxb[...] = cfb[...].astype(jnp.bfloat16).reshape(cxb.shape)
+
+    def landing(buffer):
+        return lambda at, peer: buffer.at[:, :, pl.ds(pl.multiple_of(peer * brows, brows), brows), :]
+
+    @pl.when(upper_half)
+    def _():
+        spread(lambda dest, peer: cxb.at[dest], landing(partial), 0, 0, 4)
+
+    spread(lambda dest, peer: cxb.at[dest], landing(polar.at[0]), half, 1, 3)
+
     def one_chunk(c, carry):
         pltpu.make_async_copy(lx.at[c], lx.at[c], recv_l.at[c]).wait()
         pltpu.make_async_copy(hx.at[c], hx.at[c], recv_h.at[c]).wait()
-        correlate_chunk(c, energies, lx, hx, lf, hf, cf, cx)
+        flat = (energies, rows, LANES)
+        for held, wide in ((lx, lf), (hx, hf)):
+            widen_into(wide, pl.ds(0, energies), held[c, :, :, 0].reshape(flat), held[c, :, :, 1].reshape(flat))
+        correlate_into(cf, lf, hf, lambda first: (0, (energies - first) // STEPS))
+        cx[c] = cf[...].astype(jnp.bfloat16).reshape(cx.shape[1:])
         mine = pl.ds(pl.multiple_of(me * rows, rows), rows)
 
         def push(step, carry_in):
@@ -264,7 +334,7 @@
         pltpu.make_async_copy(cx.at[c, me], polar.at[c, :, :, mine, :], recv_p.at[c]).start()
         return carry
 
-    lax.fori_loop(0, chunks, one_chunk, 0)
+    lax.fori_loop(1, chunks, one_chunk, 0)
 
     def screen(block, coupler, slot, c, begin):
         right = coupler[:, c * LANES:(c + 1) * LANES]
@@ -289,7 +359,16 @@
 
     up, down = lax.rem(row + 1, ns), lax.rem(row + ns - 1, ns)
     for c in range(chunks):
-        pltpu.make_async_copy(polar.at[c], polar.at[c], recv_p.at[c]).wait()
+        if c:
+            pltpu.make_async_copy(polar.at[c], polar.at[c], recv_p.at[c]).wait()
+        else:
+            arrived(polar.at[0], 3)
+
+            @pl.when(lower_half)
+            def _():
+                arrived(partial, 4)
+                both = polar[0].astype(jnp.float32) + partial[...].astype(jnp.float32)
+                polar[0] = both.astype(jnp.bfloat16)
 
         @pl.when(has_prev)
         def _():
@@ -327,8 +406,23 @@
         u_copy.wait_send()
 
     for kind in range(3):
-        sent = lx.at[:, pl.ds(0, n - 1)]
+        sent = lx.at[pl.ds(1, chunks - 1), pl.ds(0, n - 1)]
         pltpu.make_async_copy(sent, sent, send_sem.at[kind]).wait()
+
+    def left_here(count, kind):
+        sent = lxb.at[pl.ds(0, count)]
+        pltpu.make_async_copy(sent, sent, half_send.at[kind]).wait()
+
+    for kind in (0, 1, 3):
+        left_here(peers - 1, kind)
+
+    @pl.when(lower_half)
+    def _():
+        left_here(peers, 2)
+
+    @pl.when(upper_half)
+    def _():
+        left_here(peers, 4)
 
 
 def fused(n, ns, lesser, greater, diag, upper):
@@ -361,8 +455,16 @@
             pltpu.VMEM((size, size), bf),
             pltpu.VMEM((2, size, size), bf),
             pltpu.VMEM(whole, f32),
+            pltpu.VMEM((n, k, 2, 2 * rows, LANES), bf),
+            pltpu.VMEM((n, k, 2, 2 * rows, LANES), bf),
+            pltpu.VMEM((3, padded, 2 * rows, LANES), f32),
+            pltpu.VMEM((3, energies, 2 * rows, LANES), f32),
+            pltpu.VMEM((energies, 2, 2 * rows, LANES), f32),
+            pltpu.VMEM((n, k, 2, 2 * rows, LANES), bf),
+            pltpu.VMEM((k, 2, size, LANES), bf),
             dma((3,)), dma((3,)), dma((chunks,)), dma((chunks,)), dma((chunks,)),
             dma((2, chunks)), dma((2, chunks)), dma, dma,
+            dma((5,)), dma((5,)),
         ],
         compiler_params=pltpu.CompilerParams(
             collective_id=0, has_side_effects=True, vmem_limit_bytes=40 << 20
@@ -371,7 +473,8 @@
 
 
 def fits(n, ns, size, energies):
-    return size % n == 0 and (size // n) % 16 == 0 and size % LANES == 0 and energies % LAGS == 0 and ns > 1
+    banded = n % 2 == 0 and size % n == 0 and (size // n) % 16 == 0 and size % LANES == 0
+    return banded and size > LANES and energies % (2 * LAGS) == 0 and ns > 1
 
 
 def either(n, ns, lesser, greater, diag, upper):

time: 44.9 us -> 43.8 us (0.976); the launches traced: 44.8 us -> 43.1 us
  Pallas kernels: 44 us -> 42.2 us
    pallas_call x1, Pallas kernels: 44 us -> 42.2 us  [fused(): pl.pallas_call(functools.partial(kernel, n, ns), out_shape=jax.ShapeDtype...]
where the time goes in v3:
time: 43.8 us; the launch traced here: 43.1 us
  Pallas kernels  42.2 us (96%)
  local copies, waits for them, and re-layouts  0.8 us (2%)
    pallas_call x1, Pallas kernels, fused(): pl.pallas_call(functools.partial(kernel, n, ns), out_shape=jax.ShapeDtype...  42.2 us

profile of v3, /device:TPU:1, one launch (start us, length us, event | category | flops | bytes accessed | tf_op | source)
XLA Modules:
  0.0 43.1 jit_solution(10511390644910223353)
XLA Ops:
  0.0 42.2 %shard_map.46 = bf16[2,1,2,256,256]{4,3,2,1,0:T(8,128)(2,1)S(1)} custom-call(bf16[2,1,2,256,256]{4,3,2,1,0:T(8,128)(2,1)} %lesser.1, bf16[2,1,2,256,256]{4,3,2,1,0:T(8,128)(2,1)} %greater.1, bf16[1,256,256]{2,1,0:T(8,128)(2,1)} %diag_hbm.1, bf16[1,256,256]{2,1,0:T(8,128)(2,1)} %upper_hbm.1), custom_call_target="tpu_custom_call" | custom-call | tf_op jit(solution)/shard_map/pallas_call | solution.py:437
  42.3 0.8 %copy.6 = bf16[2,1,2,256,256]{4,3,2,1,0:T(8,128)(2,1)} copy(bf16[2,1,2,256,256]{4,3,2,1,0:T(8,128)(2,1)S(1)} %shard_map.46) | data formatting | bytes 1048576

commit v4 on v3

--- a/solution.py
+++ b/solution.py
@@ -158,7 +158,7 @@
 def kernel(
     n, ns, lesser, greater, diag_hbm, upper_hbm, out,
     diag, upper, gv, ht, lx, hx, lf, hf, cf, cx, polar, side, uprev, wside, total,
-    lxb, hxb, lfb, hfb, cfb, cxb, partial,
+    lxb, hxb, lfb, hfb, cxb, partial,
     local_sem, send_sem, recv_l, recv_h, recv_p, side_send, side_recv, u_send, u_recv, half_send, half_recv,
 ):
     me = lax.axis_index("energy")
@@ -170,7 +170,8 @@
     peers = n // 2
     half, member = me // peers, lax.rem(me, peers)
     own_energies = peers * k
-    brows = lxb.shape[3]
+    bands = lxb.shape[0]
+    brows = bands * rows
     upper_half, lower_half = half == 1, half == 0
 
     barrier = pltpu.get_barrier_semaphore()
@@ -237,31 +238,37 @@
     def _():
         u_copy.start()
 
-    def spread(pick, land, at_half, begin, kind):
+    def spread(pick, land, at_half, begin, kind, turn):
         def push(step, carry):
             peer = lax.rem(member + step, peers)
             dest = at_half * peers + peer
             pltpu.make_async_remote_copy(
                 src_ref=pick(dest, peer), dst_ref=land(me, member), send_sem=half_send.at[kind],
-                recv_sem=half_recv.at[kind], device_id=to_energy(dest), device_id_type=MESH,
+                recv_sem=half_recv.at[kind, turn], device_id=to_energy(dest), device_id_type=MESH,
             ).start()
             return carry
 
         lax.fori_loop(begin, peers, push, 0)
         if begin:
-            pltpu.make_async_copy(pick(me, member), land(me, member), half_recv.at[kind]).start()
-
-    def band(source):
-        return lambda dest, peer: source.at[
-            :, :, pl.ds(pl.multiple_of(peer * brows, brows), brows), pl.ds(0, LANES)
-        ]
+            pltpu.make_async_copy(pick(me, member), land(me, member), half_recv.at[kind, turn]).start()
+
+    def band_rows(peer, j):
+        return pl.ds(pl.multiple_of(peer * brows + j * rows, rows), rows)
+
+    def band(source, j):
+        return lambda dest, peer: source.at[:, :, band_rows(peer, j), pl.ds(0, LANES)]
+
+    def slot(buffer, j):
+        return lambda at, peer: buffer.at[j, at]
 
     @pl.when(lower_half)
     def _():
-        spread(band(ht), lambda at, peer: hxb.at[at], 1, 0, 2)
-
-    spread(band(lesser.at[:, 0]), lambda at, peer: lxb.at[at], half, 1, 0)
-    spread(band(ht), lambda at, peer: hxb.at[at], half, 1, 1)
+        for j in range(bands):
+            spread(band(ht, j), slot(hxb, j), 1, 0, 2, j)
+
+    for j in range(bands):
+        spread(band(lesser.at[:, 0], j), slot(lxb, j), half, 1, 0, j)
+        spread(band(ht, j), slot(hxb, j), half, 1, 1, j)
     for c in range(1, chunks):
         scatter(lesser.at[:, 0], lx, c, 0, recv_l)
         scatter(ht, hx, c, 1, recv_h)
@@ -275,41 +282,42 @@
         u_copy.wait_recv()
         wside[1] = uprev[...].T
 
-    def arrived(buffer, kind):
-        pltpu.make_async_copy(buffer, buffer, half_recv.at[kind]).wait()
+    def arrived(buffer, kind, turn):
+        pltpu.make_async_copy(buffer, buffer, half_recv.at[kind, turn]).wait()
 
     some = pl.ds(0, peers)
     own = pl.ds(half * peers, peers)
-    own_at = pl.ds(half * own_energies, own_energies)
-    short = (own_energies, brows, LANES)
-    arrived(lxb.at[some], 0)
-    widen_into(lfb, own_at, lxb[own, :, 0].reshape(short), lxb[own, :, 1].reshape(short))
-    arrived(hxb.at[some], 1)
-    widen_into(hfb, own_at, hxb[own, :, 0].reshape(short), hxb[own, :, 1].reshape(short))
-
-    @pl.when(upper_half)
-    def _():
-        arrived(hxb.at[some], 2)
-        widen_into(
-            hfb, pl.ds(0, own_energies), hxb[some, :, 0].reshape(short), hxb[some, :, 1].reshape(short)
-        )
+    short = (own_energies, rows, LANES)
 
     def half_bounds(first):
         begin = max(0, (own_energies - first - (LAGS + STEPS - 2)) // STEPS)
         low_end, high_end = max(0, own_energies - first) // STEPS, (energies - first) // STEPS
         return half * begin, low_end + half * (high_end - low_end)
 
-    correlate_into(cfb, lfb, hfb, half_bounds)
-    cxb[...] = cfb[...].astype(jnp.bfloat16).reshape(cxb.shape)
-
-    def landing(buffer):
-        return lambda at, peer: buffer.at[:, :, pl.ds(pl.multiple_of(peer * brows, brows), brows), :]
-
-    @pl.when(upper_half)
-    def _():
-        spread(lambda dest, peer: cxb.at[dest], landing(partial), 0, 0, 4)
-
-    spread(lambda dest, peer: cxb.at[dest], landing(polar.at[0]), half, 1, 3)
+    def landing(buffer, j):
+        return lambda at, peer: buffer.at[:, :, band_rows(peer, j), :]
+
+    for j in range(bands):
+        own_at = pl.ds(half * own_energies, own_energies)
+        arrived(lxb.at[j, some], 0, j)
+        widen_into(lfb, own_at, lxb[j, own, :, 0].reshape(short), lxb[j, own, :, 1].reshape(short))
+        arrived(hxb.at[j, some], 1, j)
+        widen_into(hfb, own_at, hxb[j, own, :, 0].reshape(short), hxb[j, own, :, 1].reshape(short))
+
+        @pl.when(upper_half)
+        def _():
+            arrived(hxb.at[j, some], 2, j)
+            re, im = hxb[j, some, :, 0].reshape(short), hxb[j, some, :, 1].reshape(short)
+            widen_into(hfb, pl.ds(0, own_energies), re, im)
+
+        correlate_into(cf, lfb, hfb, half_bounds)
+        cxb[j] = cf[...].astype(jnp.bfloat16).reshape(cxb.shape[1:])
+
+        @pl.when(upper_half)
+        def _():
+            spread(lambda dest, peer: cxb.at[j, dest], landing(partial, j), 0, 0, 4, 0)
+
+        spread(lambda dest, peer: cxb.at[j, dest], landing(polar.at[0], j), half, 1, 3, 0)
 
     def one_chunk(c, carry):
         pltpu.make_async_copy(lx.at[c], lx.at[c], recv_l.at[c]).wait()
@@ -362,11 +370,11 @@
         if c:
             pltpu.make_async_copy(polar.at[c], polar.at[c], recv_p.at[c]).wait()
         else:
-            arrived(polar.at[0], 3)
+            arrived(polar.at[0], 3, 0)
 
             @pl.when(lower_half)
             def _():
-                arrived(partial, 4)
+                arrived(partial, 4, 0)
                 both = polar[0].astype(jnp.float32) + partial[...].astype(jnp.float32)
                 polar[0] = both.astype(jnp.bfloat16)
 
@@ -410,7 +418,7 @@
         pltpu.make_async_copy(sent, sent, send_sem.at[kind]).wait()
 
     def left_here(count, kind):
-        sent = lxb.at[pl.ds(0, count)]
+        sent = lxb.at[:, pl.ds(0, count)]
         pltpu.make_async_copy(sent, sent, half_send.at[kind]).wait()
 
     for kind in (0, 1, 3):
@@ -455,16 +463,15 @@
             pltpu.VMEM((size, size), bf),
             pltpu.VMEM((2, size, size), bf),
             pltpu.VMEM(whole, f32),
-            pltpu.VMEM((n, k, 2, 2 * rows, LANES), bf),
-            pltpu.VMEM((n, k, 2, 2 * rows, LANES), bf),
-            pltpu.VMEM((3, padded, 2 * rows, LANES), f32),
-            pltpu.VMEM((3, energies, 2 * rows, LANES), f32),
-            pltpu.VMEM((energies, 2, 2 * rows, LANES), f32),
-            pltpu.VMEM((n, k, 2, 2 * rows, LANES), bf),
+            pltpu.VMEM((2, n, k, 2, rows, LANES), bf),
+            pltpu.VMEM((2, n, k, 2, rows, LANES), bf),
+            pltpu.VMEM((3, padded, rows, LANES), f32),
+            pltpu.VMEM((3, energies, rows, LANES), f32),
+            pltpu.VMEM((2, n, k, 2, rows, LANES), bf),
             pltpu.VMEM((k, 2, size, LANES), bf),
             dma((3,)), dma((3,)), dma((chunks,)), dma((chunks,)), dma((chunks,)),
             dma((2, chunks)), dma((2, chunks)), dma, dma,
-            dma((5,)), dma((5,)),
+            dma((5,)), dma((5, 2)),
         ],
         compiler_params=pltpu.CompilerParams(
             collective_id=0, has_side_effects=True, vmem_limit_bytes=40 << 20

time: 43.8 us -> 41.9 us (0.957); the launches traced: 43.1 us -> 41.7 us
  Pallas kernels: 42.2 us -> 40.9 us
    pallas_call x1, Pallas kernels: 42.2 us -> 40.9 us  [fused(): pl.pallas_call(functools.partial(kernel, n, ns), out_shape=jax.ShapeDtype...]
where the time goes in v4:
time: 41.9 us; the launch traced here: 41.7 us
  Pallas kernels  40.9 us (98%)
  local copies, waits for them, and re-layouts  0.8 us (2%)
    pallas_call x1, Pallas kernels, fused(): pl.pallas_call(functools.partial(kernel, n, ns), out_shape=jax.ShapeDtype...  40.9 us

profile of v4, /device:TPU:1, one launch (start us, length us, event | category | flops | bytes accessed | tf_op | source)
XLA Modules:
  0.0 41.7 jit_solution(3656857611177093255)
XLA Ops:
  0.0 40.9 %shard_map.46 = bf16[2,1,2,256,256]{4,3,2,1,0:T(8,128)(2,1)S(1)} custom-call(bf16[2,1,2,256,256]{4,3,2,1,0:T(8,128)(2,1)} %lesser.1, bf16[2,1,2,256,256]{4,3,2,1,0:T(8,128)(2,1)} %greater.1, bf16[1,256,256]{2,1,0:T(8,128)(2,1)} %diag_hbm.1, bf16[1,256,256]{2,1,0:T(8,128)(2,1)} %upper_hbm.1), custom_call_target="tpu_custom_call" | custom-call | tf_op jit(solution)/shard_map/pallas_call | solution.py:445
  40.9 0.8 %copy.6 = bf16[2,1,2,256,256]{4,3,2,1,0:T(8,128)(2,1)} copy(bf16[2,1,2,256,256]{4,3,2,1,0:T(8,128)(2,1)S(1)} %shard_map.46) | data formatting | bytes 1048576

commit v5 on v4

--- a/solution.py
+++ b/solution.py
@@ -266,12 +266,20 @@
         for j in range(bands):
             spread(band(ht, j), slot(hxb, j), 1, 0, 2, j)
 
-    for j in range(bands):
-        spread(band(lesser.at[:, 0], j), slot(lxb, j), half, 1, 0, j)
-        spread(band(ht, j), slot(hxb, j), half, 1, 1, j)
+    @pl.when(upper_half)
+    def _():
+        for j in range(bands):
+            spread(band(lesser.at[:, 0], j), slot(lxb, j), half, 1, 0, j)
+            spread(band(ht, j), slot(hxb, j), half, 1, 1, j)
     for c in range(1, chunks):
         scatter(lesser.at[:, 0], lx, c, 0, recv_l)
         scatter(ht, hx, c, 1, recv_h)
+
+    @pl.when(lower_half)
+    def _():
+        for j in range(bands):
+            spread(band(lesser.at[:, 0], j), slot(lxb, j), half, 1, 0, j)
+            spread(band(ht, j), slot(hxb, j), half, 1, 1, j)
 
     load_upper.wait()
     load_diag.wait()

time: 41.9 us -> 41.2 us (0.983)
  Pallas kernels: 40.9 us -> 40.2 us
    pallas_call x1, Pallas kernels: 40.9 us -> 40.2 us  [fused(): pl.pallas_call(functools.partial(kernel, n, ns), out_shape=jax.ShapeDtype...]
where the time goes in v5:
time: 41.2 us; the launch traced here: 41.1 us
  Pallas kernels  40.2 us (98%)
  local copies, waits for them, and re-layouts  0.8 us (2%)
    pallas_call x1, Pallas kernels, fused(): pl.pallas_call(functools.partial(kernel, n, ns), out_shape=jax.ShapeDtype...  40.2 us

profile of v5, /device:TPU:1, one launch (start us, length us, event | category | flops | bytes accessed | tf_op | source)
XLA Modules:
  0.0 41.1 jit_solution(3784684764058545802)
XLA Ops:
  0.0 40.2 %shard_map.46 = bf16[2,1,2,256,256]{4,3,2,1,0:T(8,128)(2,1)S(1)} custom-call(bf16[2,1,2,256,256]{4,3,2,1,0:T(8,128)(2,1)} %lesser.1, bf16[2,1,2,256,256]{4,3,2,1,0:T(8,128)(2,1)} %greater.1, bf16[1,256,256]{2,1,0:T(8,128)(2,1)} %diag_hbm.1, bf16[1,256,256]{2,1,0:T(8,128)(2,1)} %upper_hbm.1), custom_call_target="tpu_custom_call" | custom-call | tf_op jit(solution)/shard_map/pallas_call | solution.py:453
  40.3 0.8 %copy.6 = bf16[2,1,2,256,256]{4,3,2,1,0:T(8,128)(2,1)} copy(bf16[2,1,2,256,256]{4,3,2,1,0:T(8,128)(2,1)S(1)} %shard_map.46) | data formatting | bytes 1048576
